TPU v7x, 256 devices: a whole 4x4x8 slice. The times are simulated.
256 devices in a mesh: seq: 32 (over z, y), head: 8 (over x, core).
Axes of the slice: x: 4, y: 4, z: 8, core: 2. Of those that a mesh axis runs over, the one named last changes fastest.
Arguments:
- queries: bfloat16 [32768, 3072], P('seq', 'head'), may hold values from -10 to 10
- keys: bfloat16 [32768, 3072], P('seq', 'head'), may hold values from -4 to 4
- values: bfloat16 [32768, 3072], P('seq', 'head'), may hold values from -4 to 4
- w_out: bfloat16 [3072, 3072], P('head', 'seq'), may hold values from -0.21875 to 0.21875
- head_kind: int32 [24], replicated, may hold values from 0 to 1, as said below
- band_offsets: int32 [2, 7], replicated, may hold values from -4 to 4, as said below
Outputs:
- mixed: bfloat16 [32768, 3072], P(('seq', 'head'))
Inputs may be any that keep to these rules, and one draw needn't show every extreme that they name: `head_kind`: each group of 3 consecutive heads holds at most 2 temporal heads, and some group holds exactly that many. `band_offsets`: each row holds 7 distinct offsets and always contains 0, 4 and minus 4.
All inputs are finite; a program needn't handle non-finite values.
Results may differ from a plain program's by a relative error of at most 0.013.
Values may be sent and summed in bfloat16 or wider, within the bound.
A program may use at most 128 MiB of HBM per device.

v0:
```python
import math

import jax
import jax.numpy as jnp
from jax import lax
from jax.sharding import PartitionSpec as P

DH = 128
FRAMES = 16
BLK = 256


def with_halo(cells, sides, width):
    for axis, dim in sides:
        count = lax.axis_size(axis)
        ends = count - 1
        head = lax.slice_in_dim(cells, 0, width, axis=dim)
        tail = lax.slice_in_dim(cells, cells.shape[dim] - width, cells.shape[dim], axis=dim)
        cells = jnp.concatenate(
            [
                lax.ppermute(tail, axis, [(i, (i + 1) % count) for i in range(ends)]),
                cells,
                lax.ppermute(head, axis, [((i + 1) % count, i) for i in range(ends)]),
            ],
            axis=dim,
        )
    return cells


def split_shape(field_rows, seq_count):
    tok_dev, channels = field_rows.shape
    positions = tok_dev * seq_count // FRAMES
    span_rows = min(tok_dev, positions)
    return field_rows.reshape(tok_dev // span_rows, seq_count, span_rows // seq_count, channels)


def temporal_order(moved_rows):
    channels = moved_rows.shape[3]
    quota_rows = moved_rows.shape[2]
    halves = moved_rows.shape[0] // FRAMES
    grid_view = moved_rows.reshape(FRAMES, halves, quota_rows, channels)
    return grid_view.transpose(1, 2, 0, 3).reshape(halves * quota_rows * FRAMES, channels)


def frame_order(field_rows, seq_count):
    tok_dev, channels = field_rows.shape
    positions = tok_dev * seq_count // FRAMES
    span_rows = min(tok_dev, positions)
    quota_rows = span_rows // seq_count
    halves = positions // span_rows
    grid_view = field_rows.reshape(halves, quota_rows, FRAMES, channels)
    return grid_view.transpose(2, 0, 1, 3).reshape(FRAMES * halves, 1, quota_rows, channels)


def band_attend(query_rows, key_ext, value_ext, offsets, first_block, total_blocks):
    local_blocks = query_rows.shape[0] // BLK
    head_size = query_rows.shape[1]
    offset_count = offsets.shape[0]
    query_blocks = query_rows.reshape(local_blocks, BLK, head_size)
    k_blocks = key_ext.reshape(3 * local_blocks, BLK, head_size)
    v_blocks = value_ext.reshape(3 * local_blocks, BLK, head_size)
    target = jnp.arange(local_blocks, dtype=jnp.int32)[:, None] + offsets[None, :]
    global_block = first_block + target
    in_range = (global_block >= 0) & (global_block < total_blocks)
    key_index = jnp.clip(target + local_blocks, 0, 3 * local_blocks - 1)
    nearby_keys = jnp.take(k_blocks, key_index, axis=0).reshape(
        local_blocks, offset_count * BLK, head_size
    )
    nearby_values = jnp.take(v_blocks, key_index, axis=0).reshape(
        local_blocks, offset_count * BLK, head_size
    )
    score_scale = 1.0 / math.sqrt(head_size)
    attention_scores = (
        jnp.einsum("vuf,vzf->vuz", query_blocks, nearby_keys, preferred_element_type=jnp.float32)
        * score_scale
    )
    allowed = jnp.broadcast_to(in_range[:, :, None], (local_blocks, offset_count, BLK))
    allowed = allowed.reshape(local_blocks, 1, offset_count * BLK)
    attention_scores = jnp.where(allowed, attention_scores, -1e30)
    row_max = jnp.max(attention_scores, axis=2, keepdims=True)
    weights = jnp.exp(attention_scores - row_max)
    attention_probabilities = (weights / jnp.sum(weights, axis=2, keepdims=True)).astype(
        jnp.bfloat16
    )
    attended_output = jnp.einsum(
        "oyx,oxi->oyi", attention_probabilities, nearby_values, preferred_element_type=jnp.float32
    )
    return attended_output.astype(jnp.bfloat16).reshape(local_blocks * BLK, head_size)


def body(queries, keys, values, w_out, head_kind, band_offsets):
    seq_count = lax.axis_size("seq")
    seq_rank = lax.axis_index("seq")
    head_rank = lax.axis_index("head")
    tok_dev = queries.shape[0]
    head_dev = queries.shape[1] // DH
    head_types = lax.dynamic_slice_in_dim(head_kind, head_rank * head_dev, head_dev)
    is_temporal = head_types == 1
    query_heads = queries.reshape(tok_dev, head_dev, DH)
    key_heads = keys.reshape(tok_dev, head_dev, DH)
    value_heads = values.reshape(tok_dev, head_dev, DH)
    select_mask = is_temporal[None, :, None]
    moved_q, moved_k, moved_v = (
        lax.all_to_all(
            split_shape(queries, seq_count), "seq", split_axis=1, concat_axis=0, tiled=True
        ),
        lax.all_to_all(
            split_shape(keys, seq_count), "seq", split_axis=1, concat_axis=0, tiled=True
        ),
        lax.all_to_all(
            split_shape(values, seq_count), "seq", split_axis=1, concat_axis=0, tiled=True
        ),
    )
    relaid_q = temporal_order(moved_q).reshape(tok_dev, head_dev, DH)
    relaid_k = temporal_order(moved_k).reshape(tok_dev, head_dev, DH)
    relaid_v = temporal_order(moved_v).reshape(tok_dev, head_dev, DH)
    chosen_q = jnp.where(select_mask, relaid_q, query_heads)
    chosen_k = jnp.where(select_mask, relaid_k, key_heads)
    chosen_v = jnp.where(select_mask, relaid_v, value_heads)
    pair_rows = jnp.concatenate(
        [chosen_k.reshape(tok_dev, head_dev * DH), chosen_v.reshape(tok_dev, head_dev * DH)], axis=1
    )
    extended = with_halo(pair_rows, (("seq", 0),), tok_dev)
    key_ext = extended[:, : head_dev * DH].reshape(3 * tok_dev, head_dev, DH).transpose(1, 0, 2)
    value_ext = extended[:, head_dev * DH :].reshape(3 * tok_dev, head_dev, DH).transpose(1, 0, 2)
    head_offsets = jnp.where(
        is_temporal[:, None], band_offsets[1][None, :], band_offsets[0][None, :]
    )
    local_blocks = tok_dev // BLK
    first_block = seq_rank * local_blocks
    total_blocks = local_blocks * seq_count

    def attend_head(head_items):
        return band_attend(
            head_items[0], head_items[1], head_items[2], head_items[3], first_block, total_blocks
        )

    per_head = lax.map(attend_head, (chosen_q.transpose(1, 0, 2), key_ext, value_ext, head_offsets))
    attended_output = per_head.transpose(1, 0, 2)
    returned = lax.all_to_all(
        frame_order(attended_output.reshape(tok_dev, head_dev * DH), seq_count),
        "seq",
        split_axis=0,
        concat_axis=1,
        tiled=True,
    )
    returned = returned.reshape(tok_dev, head_dev, DH)
    final_rows = jnp.where(select_mask, returned, attended_output).reshape(tok_dev, head_dev * DH)
    weight_rows = lax.all_gather(w_out, "seq", axis=1, tiled=True)
    return lax.psum_scatter(
        jnp.dot(final_rows, weight_rows, preferred_element_type=jnp.float32).astype(jnp.bfloat16),
        "head",
        scatter_dimension=0,
        tiled=True,
    )


def solution(mesh):
    return jax.shard_map(
        body,
        mesh=mesh,
        in_specs=(P("seq", "head"), P("seq", "head"), P("seq", "head"), P("head", "seq"), P(), P()),
        out_specs=P(("seq", "head"), None),
        check_vma=False,
    )
```

profile of v0, /device:TPU:1, one launch (start us, length us, event | category | flops | bytes accessed | tf_op | source)
XLA Modules:
  0.0 295.6 jit_solution(4712879485724895757)
XLA Ops:
  6.5 33.2 %all_to_all.16 = bf16[1,32,32,384]{3,2,0,1:T(8,128)(2,1)S(1)} all-to-all(bf16[1,32,32,384]{3,2,0,1:T(8,128)(2,1)} %bitcast.106), channel_id=1, replica_groups=mesh['seq'=32,'head'=8] {'seq'}, dimensions={1} | all-to-all | bytes 1572864 | tf_op jit(solution)/shard_map/all_to_all | solution.py:107
  39.8 5.8 %all-to-all-start.2 = ((bf16[1,32,32,384]{3,2,0,1:T(8,128)(2,1)}), bf16[1,32,32,384]{3,2,0,1:T(8,128)(2,1)S(1)}, u32[]{:S(2)}, u32[]{:S(2)}) async-start(bf16[1,32,32,384]{3,2,0,1:T(8,128)(2,1)} %bitcast.107), calls=%async_computation.2 | async-start | bytes 1572864 | tf_op jit(solution)/shard_map/all_to_all | solution.py:110
  47.1 18.3 %all-to-all-done.2 = bf16[1,32,32,384]{3,2,0,1:T(8,128)(2,1)S(1)} async-done(((bf16[1,32,32,384]{3,2,0,1:T(8,128)(2,1)}), bf16[1,32,32,384]{3,2,0,1:T(8,128)(2,1)S(1)}, u32[]{:S(2)}, u32[]{:S(2)}) %all-to-all-start.2) | async-done | bytes 786464 | tf_op jit(solution)/shard_map/all_to_all | solution.py:110
  65.3 6.8 %all-to-all-start = ((bf16[1,32,32,384]{3,2,0,1:T(8,128)(2,1)}), bf16[1,32,32,384]{3,2,0,1:T(8,128)(2,1)}, u32[]{:S(2)}, u32[]{:S(2)}) async-start(bf16[1,32,32,384]{3,2,0,1:T(8,128)(2,1)} %bitcast.11), calls=%async_computation | async-start | bytes 1572864 | tf_op jit(solution)/shard_map/all_to_all | solution.py:104
  75.3 4.4 %collective-permute-start = (bf16[1024,768]{1,0:T(8,128)(2,1)}, bf16[1024,768]{1,0:T(8,128)(2,1)}, u32[]{:S(2)}, u32[]{:S(2)}) collective-permute-start(bf16[1024,768]{1,0:T(8,128)(2,1)} %pad_maximum_fusion.1), channel_id=1, source_target_pairs={{0,8},{8,16},{16,24},{24,32},{32,40},{40,48},{48,56},{56,64},{64,7... | collective-permute-start | bytes 4718600 | tf_op jit(solution)/shard_map/ppermute | solution.py:21
  83.5 8.4 %all-to-all-done = bf16[1,32,32,384]{3,2,0,1:T(8,128)(2,1)} async-done(((bf16[1,32,32,384]{3,2,0,1:T(8,128)(2,1)}), bf16[1,32,32,384]{3,2,0,1:T(8,128)(2,1)}, u32[]{:S(2)}, u32[]{:S(2)}) %all-to-all-start) | async-done | bytes 786464 | tf_op jit(solution)/shard_map/all_to_all | solution.py:104
  91.9 1.6 copy.30
  94.6 1.9 select_bitcast_fusion
  97.4 19.7 %collective-permute-done = bf16[1024,768]{1,0:T(8,128)(2,1)} collective-permute-done((bf16[1024,768]{1,0:T(8,128)(2,1)}, bf16[1024,768]{1,0:T(8,128)(2,1)}, u32[]{:S(2)}, u32[]{:S(2)}) %collective-permute-start) | collective-permute-done | bytes 1572896 | tf_op jit(solution)/shard_map/ppermute | solution.py:21
  117.2 3.6 %collective-permute-done.1 = bf16[1024,768]{1,0:T(8,128)(2,1)} collective-permute-done((bf16[1024,768]{1,0:T(8,128)(2,1)}, bf16[1024,768]{1,0:T(8,128)(2,1)}, u32[]{:S(2)}, u32[]{:S(2)}) %collective-permute-start.1) | collective-permute-done | bytes 1572896 | tf_op jit(solution)/shard_map/ppermute | solution.py:23
  120.7 3.0 %pad_maximum_fusion = bf16[3072,768]{1,0:T(8,128)(2,1)S(1)} fusion(bf16[1024,768]{1,0:T(8,128)(2,1)} %collective-permute-done.1, bf16[1024,384]{1,0:T(8,128)(2,1)S(1)} %get-tuple-element.92, bf16[1024,384]{1,0:T(8,128)(2,1)S(1)} %get-tuple-element.91, bf16[1024,768]{1,0:T(8,128)(2,1)} %collective-permute-done), kind=kLoop, calls=%fused_computation.33 | loop fusion | flops 18874368 | bytes 9437184 | tf_op jit(solution)/shard_map/concatenate | solution.py:19
  123.7 1.9 fusion.17
  125.6 4.3 %copy.35 = bf16[3072,384]{0,1:T(8,128)(2,1)} copy(bf16[3072,384]{1,0:T(8,128)(2,1)} %get-tuple-element.88) | data formatting | bytes 4718592 | tf_op jit(solution)/shard_map/slice | solution.py:124
  129.9 2.6 copy.36
  132.5 66.0 %while.10 = (s32[]{:T(128)}, bf16[3,1024,128]{2,1,0:T(8,128)(2,1)}, s32[]{:T(128)}, s32[3,7]{1,0:T(4,128)S(1)}, bf16[3,1024,128]{2,1,0:T(8,128)(2,1)}, /*index=5...) while((s32[]{:T(128)}, bf16[3,1024,128]{2,1,0:T(8,128)(2,1)}, s32[]{:T(128)}, ...), condition=%wide.region_3.5_spmd, body=%wide.region_0.4_spmd.sunk | while | flops 952503552 | bytes 48276992 | solution.py:138
  135.8 2.1 gather_fusion.1
  137.9 3.7 %broadcast_select_fusion.5 = (bf16[4,7,256,128]{3,2,1,0:T(8,128)(2,1)}, bf16[4,7,256,128]{3,2,1,0:T(8,128)(2,1)}) fusion(bf16[4,7,256,128]{3,2,1,0:T(8,128)(2,1)S(1)} %bitcast.97, pred[4,7]{1,0:T(4,128)(4,1)S(1)} %get-tuple-element.145, bf16[4,7,256,128]{3,2,1,0:T(8,128)(2,1)} %bitcast.98), kind=kLoop, calls=%fused_computation.12.clone.1 | loop fusion | flops 1835008 | bytes 7340060 | tf_op jit(solution)/shard_map/while/body/eval_jaxpr/jit(_take)/select_n | solution.py:66
  142.7 6.9 %fusion.37 = (f32[4,256]{1,0:T(4,128)S(1)}, f32[4,256,1792]{2,1,0:T(8,128)}) fusion(pred[4,1792]{1,0:T(4,128)(4,1)S(1)} %bitcast.114, bf16[4,256,128]{2,1,0:T(8,128)(2,1)S(1)} %bitcast.103, bf16[4,1792,128]{2,1,0:T(8,128)(2,1)} %bitcast.100), kind=kOutput, calls=%fused_computation.45.clone.1 | convolution fusion | flops 477103872 | bytes 9448448 | tf_op jit(solution)/shard_map/while/body/eval_jaxpr/sub | solution.py:81
  149.6 4.3 %fusion.38 = bf16[4,256,128]{2,1,0:T(8,128)(2,1)S(1)} fusion(bf16[4,1792,128]{2,1,0:T(8,128)(2,1)S(1)} %bitcast.99, f32[4,256,1792]{2,1,0:T(8,128)} %get-tuple-element.150, f32[4,256]{1,0:T(4,128)S(1)} %get-tuple-element.151), kind=kOutput, calls=%fused_computation.13.clone.1 | convolution fusion | flops 473563136 | bytes 9441280 | tf_op jit(solution)/shard_map/while/body/eval_jaxpr/oyx,oxi->oyi/dot_general | solution.py:85
  154.6 1.5 constant_dynamic-slice_fusion.6
  157.9 2.1 gather_fusion.1
  159.9 3.7 %broadcast_select_fusion.5 = (bf16[4,7,256,128]{3,2,1,0:T(8,128)(2,1)}, bf16[4,7,256,128]{3,2,1,0:T(8,128)(2,1)}) fusion(bf16[4,7,256,128]{3,2,1,0:T(8,128)(2,1)S(1)} %bitcast.97, pred[4,7]{1,0:T(4,128)(4,1)S(1)} %get-tuple-element.145, bf16[4,7,256,128]{3,2,1,0:T(8,128)(2,1)} %bitcast.98), kind=kLoop, calls=%fused_computation.12.clone.1 | loop fusion | flops 1835008 | bytes 7340060 | tf_op jit(solution)/shard_map/while/body/eval_jaxpr/jit(_take)/select_n | solution.py:66
  164.7 6.9 %fusion.37 = (f32[4,256]{1,0:T(4,128)S(1)}, f32[4,256,1792]{2,1,0:T(8,128)}) fusion(pred[4,1792]{1,0:T(4,128)(4,1)S(1)} %bitcast.114, bf16[4,256,128]{2,1,0:T(8,128)(2,1)S(1)} %bitcast.103, bf16[4,1792,128]{2,1,0:T(8,128)(2,1)} %bitcast.100), kind=kOutput, calls=%fused_computation.45.clone.1 | convolution fusion | flops 477103872 | bytes 9448448 | tf_op jit(solution)/shard_map/while/body/eval_jaxpr/sub | solution.py:81
  171.6 4.3 %fusion.38 = bf16[4,256,128]{2,1,0:T(8,128)(2,1)S(1)} fusion(bf16[4,1792,128]{2,1,0:T(8,128)(2,1)S(1)} %bitcast.99, f32[4,256,1792]{2,1,0:T(8,128)} %get-tuple-element.150, f32[4,256]{1,0:T(4,128)S(1)} %get-tuple-element.151), kind=kOutput, calls=%fused_computation.13.clone.1 | convolution fusion | flops 473563136 | bytes 9441280 | tf_op jit(solution)/shard_map/while/body/eval_jaxpr/oyx,oxi->oyi/dot_general | solution.py:85
  179.8 2.1 gather_fusion.1
  181.9 3.7 %broadcast_select_fusion.5 = (bf16[4,7,256,128]{3,2,1,0:T(8,128)(2,1)}, bf16[4,7,256,128]{3,2,1,0:T(8,128)(2,1)}) fusion(bf16[4,7,256,128]{3,2,1,0:T(8,128)(2,1)S(1)} %bitcast.97, pred[4,7]{1,0:T(4,128)(4,1)S(1)} %get-tuple-element.145, bf16[4,7,256,128]{3,2,1,0:T(8,128)(2,1)} %bitcast.98), kind=kLoop, calls=%fused_computation.12.clone.1 | loop fusion | flops 1835008 | bytes 7340060 | tf_op jit(solution)/shard_map/while/body/eval_jaxpr/jit(_take)/select_n | solution.py:66
  186.7 6.9 %fusion.37 = (f32[4,256]{1,0:T(4,128)S(1)}, f32[4,256,1792]{2,1,0:T(8,128)}) fusion(pred[4,1792]{1,0:T(4,128)(4,1)S(1)} %bitcast.114, bf16[4,256,128]{2,1,0:T(8,128)(2,1)S(1)} %bitcast.103, bf16[4,1792,128]{2,1,0:T(8,128)(2,1)} %bitcast.100), kind=kOutput, calls=%fused_computation.45.clone.1 | convolution fusion | flops 477103872 | bytes 9448448 | tf_op jit(solution)/shard_map/while/body/eval_jaxpr/sub | solution.py:81
  193.5 4.3 %fusion.38 = bf16[4,256,128]{2,1,0:T(8,128)(2,1)S(1)} fusion(bf16[4,1792,128]{2,1,0:T(8,128)(2,1)S(1)} %bitcast.99, f32[4,256,1792]{2,1,0:T(8,128)} %get-tuple-element.150, f32[4,256]{1,0:T(4,128)S(1)} %get-tuple-element.151), kind=kOutput, calls=%fused_computation.13.clone.1 | convolution fusion | flops 473563136 | bytes 9441280 | tf_op jit(solution)/shard_map/while/body/eval_jaxpr/oyx,oxi->oyi/dot_general | solution.py:85
  198.5 1.8 copy.50
  201.3 34.8 %all_to_all.17 = bf16[32,1,32,384]{3,2,1,0:T(8,128)(2,1)S(1)} all-to-all(bf16[32,1,32,384]{3,2,1,0:T(8,128)(2,1)S(1)} %bitcast.112), channel_id=1, replica_groups=mesh['seq'=32,'head'=8] {'seq'}, dimensions={0} | all-to-all | bytes 1572864 | tf_op jit(solution)/shard_map/all_to_all | solution.py:140
  237.8 7.1 %convolution_convert_fusion = bf16[1024,3072]{1,0:T(8,128)(2,1)} fusion(bf16[1024,384]{0,1:T(8,128)(2,1)S(1)} %bitcast.113, bf16[384,3072]{0,1:T(8,128)(2,1)} %all-gather.2.cloned.1.call-done), kind=kOutput, calls=%fused_computation.32 | convolution fusion | flops 2419064832 | bytes 9437184 | tf_op jit(solution)/shard_map/dot_general | solution.py:151
  244.9 43.8 %reduce-scatter.2.cloned.1.call-done = bf16[128,3072]{1,0:T(8,128)(2,1)} async-done(((bf16[1024,3072]{1,0:T(8,128)(2,1)}), bf16[128,3072]{1,0:T(8,128)(2,1)}) %reduce-scatter.2.cloned.1.call-update) | async-done | bytes 786448 | tf_op jit(solution)/shard_map/reduce_scatter | solution.py:150
  (78 shorter events, 26.8 us)
Async XLA Ops:
  6.5 39.0 %copy-start.5 = (s32[24]{0:T(128)S(1)}, s32[24]{0:T(128)}, u32[]{:S(2)}) copy-start(s32[24]{0:T(128)} %param.14) | copy-start | bytes 292
  39.8 25.6 %all-to-all-start.2 = ((bf16[1,32,32,384]{3,2,0,1:T(8,128)(2,1)}), bf16[1,32,32,384]{3,2,0,1:T(8,128)(2,1)S(1)}, u32[]{:S(2)}, u32[]{:S(2)}) async-start(bf16[1,32,32,384]{3,2,0,1:T(8,128)(2,1)} %bitcast.107), calls=%async_computation.2 | async-start | bytes 1572864 | tf_op jit(solution)/shard_map/all_to_all | solution.py:110
  45.7 26.9 %copy-start.1 = (bf16[1024,384]{1,0:T(8,128)(2,1)S(1)}, bf16[1024,384]{1,0:T(8,128)(2,1)}, u32[]{:S(2)}) copy-start(bf16[1024,384]{1,0:T(8,128)(2,1)} %param.11) | copy-start | bytes 2359300
  45.7 26.9 %copy-start.2 = (bf16[1024,384]{1,0:T(8,128)(2,1)S(1)}, bf16[1024,384]{1,0:T(8,128)(2,1)}, u32[]{:S(2)}) copy-start(bf16[1024,384]{1,0:T(8,128)(2,1)} %param.12) | copy-start | bytes 2359300
  65.3 26.5 %all-to-all-start = ((bf16[1,32,32,384]{3,2,0,1:T(8,128)(2,1)}), bf16[1,32,32,384]{3,2,0,1:T(8,128)(2,1)}, u32[]{:S(2)}, u32[]{:S(2)}) async-start(bf16[1,32,32,384]{3,2,0,1:T(8,128)(2,1)} %bitcast.11), calls=%async_computation | async-start | bytes 1572864 | tf_op jit(solution)/shard_map/all_to_all | solution.py:104
  72.1 165.6 %all-gather.2.cloned.1.call-start = ((), (), s32[]{:S(2)}) async-start(), calls=%async_computation.5 | async-start | bytes 2433024 | tf_op jit(solution)/shard_map/all_gather | solution.py:149
  75.3 8.1 %copy-start.4 = (s32[2,7]{1,0:T(2,128)S(1)}, s32[2,7]{1,0:T(2,128)}, u32[]{:S(2)}) copy-start(s32[2,7]{1,0:T(2,128)} %param.15) | copy-start | bytes 172
  75.3 41.9 %collective-permute-start = (bf16[1024,768]{1,0:T(8,128)(2,1)}, bf16[1024,768]{1,0:T(8,128)(2,1)}, u32[]{:S(2)}, u32[]{:S(2)}) collective-permute-start(bf16[1024,768]{1,0:T(8,128)(2,1)} %pad_maximum_fusion.1), channel_id=1, source_target_pairs={{0,8},{8,16},{16,24},{24,32},{32,40},{40,48},{48,56},{56,64},{64,7... | collective-permute-start | bytes 4718600 | tf_op jit(solution)/shard_map/ppermute | solution.py:21
  79.7 41.1 %collective-permute-start.1 = (bf16[1024,768]{1,0:T(8,128)(2,1)}, bf16[1024,768]{1,0:T(8,128)(2,1)}, u32[]{:S(2)}, u32[]{:S(2)}) collective-permute-start(bf16[1024,768]{1,0:T(8,128)(2,1)} %pad_maximum_fusion.1), channel_id=1, source_target_pairs={{8,0},{16,8},{24,16},{32,24},{40,32},{48,40},{56,48},{64,56},{72,6... | collective-permute-start | bytes 4718600 | tf_op jit(solution)/shard_map/ppermute | solution.py:23
  81.0 207.8 %reduce-scatter.2.cloned.1.call-start = ((), (), s32[]{:S(2)}) async-start(), calls=%async_computation.6 | async-start | bytes 7077888 | tf_op jit(solution)/shard_map/reduce_scatter | solution.py:150
  142.7 6.9 %copy-start = (bf16[4,7,256,128]{3,2,1,0:T(8,128)(2,1)S(1)}, bf16[4,7,256,128]{3,2,1,0:T(8,128)(2,1)}, u32[]{:S(2)}) copy-start(bf16[4,7,256,128]{3,2,1,0:T(8,128)(2,1)} %get-tuple-element.147) | copy-start | bytes 5505028 | tf_op jit(solution)/shard_map/while
  164.7 6.9 %copy-start = (bf16[4,7,256,128]{3,2,1,0:T(8,128)(2,1)S(1)}, bf16[4,7,256,128]{3,2,1,0:T(8,128)(2,1)}, u32[]{:S(2)}) copy-start(bf16[4,7,256,128]{3,2,1,0:T(8,128)(2,1)} %get-tuple-element.147) | copy-start | bytes 5505028 | tf_op jit(solution)/shard_map/while
  186.7 6.9 %copy-start = (bf16[4,7,256,128]{3,2,1,0:T(8,128)(2,1)S(1)}, bf16[4,7,256,128]{3,2,1,0:T(8,128)(2,1)}, u32[]{:S(2)}) copy-start(bf16[4,7,256,128]{3,2,1,0:T(8,128)(2,1)} %get-tuple-element.147) | copy-start | bytes 5505028 | tf_op jit(solution)/shard_map/while
  201.1 35.2 %copy-start.3 = (bf16[3,1024,128]{2,1,0:T(8,128)(2,1)S(1)}, bf16[3,1024,128]{2,1,0:T(8,128)(2,1)}, u32[]{:S(2)}) copy-start(bf16[3,1024,128]{2,1,0:T(8,128)(2,1)} %get-tuple-element.43) | copy-start | bytes 2359300
Sparse Core Ops, SparseCore 0:
  81.1 78.3 all-gather.1
  245.0 43.6 reduce-scatter.1
where the time goes:
time: 297 us; the launch traced here: 296 us
  waiting for transfers between devices  93.8 us (32%)
  blocking collectives  68 us (23%)
  local copies, waits for them, and re-layouts  41.4 us (14%)
  matrix products  40.5 us (14%)
  other arithmetic  19.6 us (7%)
  starting transfers between devices  18.5 us (6%)
  between operations  13.6 us (5%)
    reduce_scatter x1, waiting for transfers between devices, body(): lax.psum_scatter(jnp.dot(final_rows, weight_rows, preferred_element_type=...  43.8 us
    all_to_all x1, blocking collectives, body(): lax.all_to_all(frame_order(attended_output.reshape(tok_dev, head_dev * DH...  34.8 us
    all_to_all x1, blocking collectives, body(): lax.all_to_all(split_shape(keys, seq_count), 'seq', split_axis=1, concat_...  33.2 us
    sub x3, matrix products, band_attend(): weights = jnp.exp(attention_scores - row_max)  20.6 us
    ppermute x1, waiting for transfers between devices, with_halo(): lax.ppermute(tail, axis, [(i, (i + 1) % count) for i in range(ends)])  19.7 us
    all_to_all x1, waiting for transfers between devices, body(): lax.all_to_all(split_shape(values, seq_count), 'seq', split_axis=1, conca...  18.3 us
    dot_general x3, matrix products, band_attend(): jnp.einsum('oyx,oxi->oyi', attention_probabilities, nearby_values, prefer...  12.8 us
    select_n x6, other arithmetic, band_attend(): jnp.take(k_blocks, key_index, axis=0)  11.1 us
  transfers between devices with their start and end apart: 6, of which 5 were waited for; matrix products, arithmetic and copies ran while one was open for 32% of the time, Pallas kernels for 0%

commit v1 on v0

v1 whole, which is shorter than its diff:
```python
import math

import jax
import jax.numpy as jnp
from jax import lax
from jax.experimental import pallas as pl
from jax.experimental.pallas import tpu as pltpu
from jax.sharding import PartitionSpec as P

DH = 128
BLK = 256
NS = 32
KOFF = 7
BF = jnp.bfloat16
F32 = jnp.float32
MESH = pl.DeviceIdType.MESH
EXP_SCALE = math.log2(math.e) / math.sqrt(DH)


def pick(cond, yes, no):
    return jnp.where(cond, yes, no)


def kernel(kind_ref, offs_ref, q_ref, k_ref, v_ref, out_ref,
           snd, rcv, qx, kv0, kv1, kv2, att, ret,
           snd_sem, rcv_sem, halo_send, halo_recv, ret_send, ret_recv):
    s = lax.axis_index("seq")
    g = lax.axis_index("head")
    frame = s // 2
    half = s % 2
    kvs = (kv0, kv1, kv2)

    barrier = pltpu.get_barrier_semaphore()

    def greet(i, c):
        pl.semaphore_signal(barrier, inc=1, device_id={"seq": lax.rem(s + i, NS)}, device_id_type=MESH)
        return c

    lax.fori_loop(1, NS, greet, 0)

    kinds = [kind_ref[g * 3 + i] for i in range(3)]
    sp0 = kinds[0] == 0
    sp2 = jnp.logical_and(kinds[0] != 0, kinds[1] != 0)
    sp1 = jnp.logical_and(kinds[0] != 0, kinds[1] == 0)
    kind_slot = (jnp.where(sp0, kinds[1], kinds[0]), jnp.where(sp2, kinds[1], kinds[2]), 0)

    srcs = (q_ref, k_ref, v_ref)

    def prep(r, c):
        rows = pl.ds(pl.multiple_of(r * 128, 128), 128)
        for t in range(3):
            a = srcs[t][rows, 0:128]
            b = srcs[t][rows, 128:256]
            d = srcs[t][rows, 256:384]
            x0 = pick(sp0, b, a)
            x1 = pick(sp2, b, d)
            snd[0, pl.ds(r * 4, 4), t] = x0.reshape(4, 2, 16, DH)
            snd[1, pl.ds(r * 4, 4), t] = x1.reshape(4, 2, 16, DH)
            x2 = pick(sp0, a, pick(sp2, d, b)).reshape(8, 16, DH)
            blk = r // 2
            part = pl.ds((r % 2) * 8, 8)
            if t == 0:
                qx[2, blk, part] = x2
            else:
                kv2[t - 1, 4 + blk, part] = x2
        return c

    lax.fori_loop(0, 8, prep, 0)
    pl.semaphore_wait(barrier, NS - 1)

    def scatter(slot):
        def go(i, c):
            d = lax.rem(s + i, NS)
            pltpu.make_async_remote_copy(
                src_ref=snd.at[slot, d],
                dst_ref=rcv.at[slot, :, pl.ds(half * 2, 2), frame],
                send_sem=snd_sem.at[slot], recv_sem=rcv_sem.at[slot],
                device_id={"seq": d}, device_id_type=MESH).start()
            return c
        lax.fori_loop(1, NS, go, 0)
        pltpu.make_async_copy(
            snd.at[slot, s], rcv.at[slot, :, pl.ds(half * 2, 2), frame], rcv_sem.at[slot]).start()

    def halo(slot):
        kv = kvs[slot]
        ops = []
        for side in range(2):
            peer = lax.rem(s + (1 if side == 0 else NS - 1), NS)
            lo = 0 if side == 0 else 8
            op = pltpu.make_async_remote_copy(
                src_ref=kv.at[:, pl.ds(4, 4)],
                dst_ref=kv.at[:, pl.ds(lo, 4)],
                send_sem=halo_send.at[slot, side], recv_sem=halo_recv.at[slot, side],
                device_id={"seq": peer}, device_id_type=MESH)
            op.start()
            ops.append(op)
        return ops

    scatter(0)
    halo2 = halo(2)
    scatter(1)

    def attend(slot):
        kv = kvs[slot]
        offs = [jnp.where(kind_slot[slot] == 1, offs_ref[1, o], offs_ref[0, o]) for o in range(KOFF)]
        ones = jnp.ones((BLK, DH), BF)

        def block(j, c):
            q = qx[slot, j].reshape(BLK, DH)
            ks, vs, pens = [], [], []
            for o in range(KOFF):
                t = j + offs[o]
                gb = s * 4 + t
                ok = jnp.logical_and(gb >= 0, gb < NS * 4)
                idx = jnp.where(ok, t + 4, j + 4)
                ks.append(kv[0, idx].reshape(BLK, DH))
                vs.append(jnp.concatenate([kv[1, idx].reshape(BLK, DH), ones], axis=1))
                pens.append(jnp.where(ok, 0.0, 1e30).astype(F32))
            sc = [lax.dot_general(q, k, (((1,), (1,)), ((), ())), preferred_element_type=F32) for k in ks]
            m = sc[0]
            for x in sc[1:]:
                m = jnp.maximum(m, x)
            mx = jnp.max(m, axis=1, keepdims=True) * EXP_SCALE
            ps = [jnp.exp2(x * EXP_SCALE - (mx + pen)).astype(BF) for x, pen in zip(sc, pens)]
            acc = jnp.dot(jnp.concatenate(ps, axis=1), jnp.concatenate(vs, axis=0),
                          preferred_element_type=F32)
            o = (acc[:, :DH] / acc[:, DH:]).astype(BF)
            att[slot, j] = o.reshape(16, 16, DH)
            return c

        lax.fori_loop(0, 4, block, 0)

    def wait_halo(ops):
        for op in ops:
            op.wait()

    def arrive(slot):
        pltpu.make_async_copy(rcv.at[slot], rcv.at[slot], rcv_sem.at[slot]).wait()
        temporal = kind_slot[slot] == 1

        def sel(b, c):
            for t in range(3):
                local = snd[slot, pl.ds(b * 8, 8), t].reshape(16, 16, DH)
                x = pick(temporal, rcv[slot, t, b], local)
                if t == 0:
                    qx[slot, b] = x
                else:
                    kvs[slot][t - 1, 4 + b] = x
            return c

        lax.fori_loop(0, 4, sel, 0)

    def give_back(slot):
        def go(i, c):
            d = lax.rem(s + i, NS)
            pltpu.make_async_remote_copy(
                src_ref=att.at[slot, pl.ds((d % 2) * 2, 2), d // 2],
                dst_ref=ret.at[slot, s],
                send_sem=ret_send.at[slot], recv_sem=ret_recv.at[slot],
                device_id={"seq": d}, device_id_type=MESH).start()
            return c
        lax.fori_loop(1, NS, go, 0)
        pltpu.make_async_copy(
            att.at[slot, pl.ds(half * 2, 2), frame], ret.at[slot, s], ret_recv.at[slot]).start()

    wait_halo(halo2)
    attend(2)
    arrive(0)
    halo0 = halo(0)
    arrive(1)
    halo1 = halo(1)
    wait_halo(halo0)
    attend(0)
    give_back(0)
    wait_halo(halo1)
    attend(1)
    give_back(1)

    def finish2(b, c):
        out_ref[pl.ds(pl.multiple_of(b * BLK, BLK), BLK), 256:384] = att[2, b].reshape(BLK, DH)
        return c

    lax.fori_loop(0, 4, finish2, 0)

    for slot in range(2):
        pltpu.make_async_copy(ret.at[slot], ret.at[slot], ret_recv.at[slot]).wait()
        temporal = kind_slot[slot] == 1

        def fin(b, c):
            x = pick(temporal, ret[slot, pl.ds(b * 8, 8)].reshape(BLK, DH), att[slot, b].reshape(BLK, DH))
            out_ref[pl.ds(pl.multiple_of(b * BLK, BLK), BLK), slot * DH:(slot + 1) * DH] = x
            return c

        lax.fori_loop(0, 4, fin, 0)

    for slot in range(2):
        sent = snd.at[slot, pl.ds(0, NS - 1)]
        pltpu.make_async_copy(sent, sent, snd_sem.at[slot]).wait()
        back = ret.at[slot, pl.ds(0, NS - 1)]
        pltpu.make_async_copy(back, back, ret_send.at[slot]).wait()


def attention(queries, keys, values, head_kind, band_offsets):
    vm = pl.BlockSpec(memory_space=pltpu.VMEM)
    sm = pl.BlockSpec(memory_space=pltpu.SMEM)
    dma = pltpu.SemaphoreType.DMA
    return pl.pallas_call(
        kernel,
        out_shape=jax.ShapeDtypeStruct((1024, 384), BF),
        in_specs=[sm, sm, vm, vm, vm],
        out_specs=vm,
        scratch_shapes=[
            pltpu.VMEM((2, NS, 3, 2, 16, DH), BF),
            pltpu.VMEM((2, 3, 4, 16, 16, DH), BF),
            pltpu.VMEM((3, 4, 16, 16, DH), BF),
            pltpu.VMEM((2, 12, 16, 16, DH), BF),
            pltpu.VMEM((2, 12, 16, 16, DH), BF),
            pltpu.VMEM((2, 12, 16, 16, DH), BF),
            pltpu.VMEM((3, 4, 16, 16, DH), BF),
            pltpu.VMEM((2, NS, 2, 16, DH), BF),
            dma((2,)), dma((2,)), dma((3, 2)), dma((3, 2)), dma((2,)), dma((2,)),
        ],
        compiler_params=pltpu.CompilerParams(
            collective_id=0, has_side_effects=True, vmem_limit_bytes=60 * 1024 * 1024),
    )(head_kind, band_offsets, queries, keys, values)


def body(queries, keys, values, w_out, head_kind, band_offsets):
    head_rank = lax.axis_index("head")
    types = lax.dynamic_slice_in_dim(head_kind, head_rank * 3, 3)
    a, b, d = w_out[0:DH], w_out[DH:2 * DH], w_out[2 * DH:]
    sp0 = types[0] == 0
    sp2 = (types[0] != 0) & (types[1] != 0)
    rows = jnp.concatenate(
        [jnp.where(sp0, b, a), jnp.where(sp2, b, d), jnp.where(sp0, a, jnp.where(sp2, d, b))], axis=0)
    weight_rows = lax.all_gather(rows, "seq", axis=1, tiled=True)
    final_rows = attention(queries, keys, values, head_kind, band_offsets)
    return lax.psum_scatter(
        jnp.dot(final_rows, weight_rows, preferred_element_type=F32).astype(BF),
        "head", scatter_dimension=0, tiled=True)


def solution(mesh):
    return jax.shard_map(
        body,
        mesh=mesh,
        in_specs=(P("seq", "head"), P("seq", "head"), P("seq", "head"), P("head", "seq"), P(), P()),
        out_specs=P(("seq", "head"), None),
        check_vma=False,
    )
```

time: 297 us -> 186 us (0.63)
  Pallas kernels: 0 us -> 107 us
  blocking collectives: 68 us -> 0 us
  waiting for transfers between devices: 93.8 us -> 52.3 us
  local copies, waits for them, and re-layouts: 41.4 us -> 1.31 us
  matrix products: 40.5 us -> 8.02 us
  starting transfers between devices: 18.5 us -> 0.04 us
  other arithmetic: 19.6 us -> 1.43 us
    pallas_call x0 -> x1, Pallas kernels: none -> 107 us  [attention(): pl.pallas_call(kernel, out_shape=jax.ShapeDtypeStruct((1024, 384), BF), i...]
    all_to_all x2 -> x0, blocking collectives: 68 us -> none  [the longest x1 34.8 us: body(): lax.all_to_all(frame_order(attended_output.reshape(tok_dev, head_dev * DH...]
    all_to_all x2 -> x0, waiting for transfers between devices: 26.6 us -> none  [the longest x1 18.3 us: body(): lax.all_to_all(split_shape(values, seq_count), 'seq', split_axis=1, conca...]
    ppermute x2 -> x0, waiting for transfers between devices: 23.3 us -> none  [the longest x1 19.7 us: with_halo(): lax.ppermute(tail, axis, [(i, (i + 1) % count) for i in range(ends)])]
    sub x3 -> x0, matrix products: 20.6 us -> none  [band_attend(): weights = jnp.exp(attention_scores - row_max)]
    select_n x9 -> x1, other arithmetic: 13.4 us -> 0.79 us  [body(): jnp.where(sp0, b, a)]
    all_to_all x2 -> x0, starting transfers between devices: 12.6 us -> none  [the longest x1 6.8 us: body(): lax.all_to_all(split_shape(queries, seq_count), 'seq', split_axis=1, conc...]
    dot_general x4 -> x1, matrix products: 19.9 us -> 8.02 us  [body(): jnp.dot(final_rows, weight_rows, preferred_element_type=F32).astype(BF)]
  transfers between devices with their start and end apart: 6 -> 2, of which waited for: 5 -> 2; matrix products, arithmetic and copies ran while one was open for 32% -> 0% of each run, Pallas kernels for 0% -> 58%
where the time goes in v1:
time: 186 us
  Pallas kernels  107 us (58%)
  waiting for transfers between devices  52.3 us (28%)
  between operations  15.2 us (8%)
  matrix products  8.02 us (4%)
    pallas_call x1, Pallas kernels, attention(): pl.pallas_call(kernel, out_shape=jax.ShapeDtypeStruct((1024, 384), BF), i...  107 us
    reduce_scatter x1, waiting for transfers between devices, body(): lax.psum_scatter(jnp.dot(final_rows, weight_rows, preferred_element_type=...  45.7 us
    dot_general x1, matrix products, body(): jnp.dot(final_rows, weight_rows, preferred_element_type=F32).astype(BF)  8.02 us
    all_gather x1, waiting for transfers between devices, body(): weight_rows = lax.all_gather(rows, 'seq', axis=1, tiled=True)  6.49 us
  transfers between devices with their start and end apart: 2, of which 2 were waited for; matrix products, arithmetic and copies ran while one was open for 0% of the time, Pallas kernels for 58%

profile of v1, /device:TPU:1, one launch (start us, length us, event | category | flops | bytes accessed | tf_op | source)
XLA Modules:
  0.0 185.7 jit_solution(14624029435731403888)
XLA Ops:
  6.5 0.0 all-gather.2.cloned.1.call-start
  6.5 0.7 dynamic_slice.3
  7.3 0.6 fusion
  9.6 0.8 broadcast_select_fusion.1
  10.4 0.6 pad_maximum_fusion
  11.1 0.0 all-gather.2.cloned.1.call-update
  11.1 0.0 reduce-scatter.2.cloned.1.call-start
  11.1 107.4 %shard_map.64 = bf16[1024,384]{1,0:T(8,128)(2,1)} custom-call(s32[24]{0:T(128)} %kind_ref.1, s32[2,7]{1,0:T(2,128)} %offs_ref.1, bf16[1024,384]{1,0:T(8,128)(2,1)} %q_ref.1, bf16[1024,384]{1,0:T(8,128)(2,1)} %k_ref.1, bf16[1024,384]{1,0:T(8,128)(2,1)} %v_ref.1), custom_call_target="tpu_custom_call" | custom-call | tf_op jit(solution)/shard_map/pallas_call | solution.py:207
  118.6 6.5 %all-gather.2.cloned.1.call-done = bf16[384,3072]{0,1:T(8,128)(2,1)} async-done(((bf16[384,96]{0,1:T(8,128)(2,1)}), bf16[384,3072]{0,1:T(8,128)(2,1)}) %all-gather.2.cloned.1.call-update) | async-done | bytes 2359312 | tf_op jit(solution)/shard_map/all_gather | solution.py:236
  125.1 8.0 %convolution_convert_fusion = bf16[1024,3072]{1,0:T(8,128)(2,1)} fusion(bf16[1024,384]{1,0:T(8,128)(2,1)} %shard_map.64, bf16[384,3072]{0,1:T(8,128)(2,1)} %all-gather.2.cloned.1.call-done), kind=kOutput, calls=%fused_computation | convolution fusion | flops 2419064832 | bytes 9437184 | tf_op jit(solution)/shard_map/dot_general | solution.py:239
  133.1 0.0 reduce-scatter.2.cloned.1.call-update
  133.1 45.7 %reduce-scatter.2.cloned.1.call-done = bf16[128,3072]{1,0:T(8,128)(2,1)} async-done(((bf16[1024,3072]{1,0:T(8,128)(2,1)}), bf16[128,3072]{1,0:T(8,128)(2,1)}) %reduce-scatter.2.cloned.1.call-update) | async-done | bytes 786448 | tf_op jit(solution)/shard_map/reduce_scatter | solution.py:238
Async XLA Ops:
  6.5 118.5 %all-gather.2.cloned.1.call-start = ((), (), s32[]{:S(2)}) async-start(), calls=%async_computation.1 | async-start | bytes 2433024 | tf_op jit(solution)/shard_map/all_gather | solution.py:236
  11.1 167.8 %reduce-scatter.2.cloned.1.call-start = ((), (), s32[]{:S(2)}) async-start(), calls=%async_computation.2 | async-start | bytes 7077888 | tf_op jit(solution)/shard_map/reduce_scatter | solution.py:238
Sparse Core Ops, SparseCore 0:
  11.2 113.8 all-gather.1
  133.2 45.5 reduce-scatter.1

commit v2 on v1

--- a/solution.py
+++ b/solution.py
@@ -21,13 +21,22 @@
     return jnp.where(cond, yes, no)
 
 
-def kernel(kind_ref, offs_ref, q_ref, k_ref, v_ref, out_ref,
-           snd, rcv, qx, kv0, kv1, kv2, att, ret,
-           snd_sem, rcv_sem, halo_send, halo_recv, ret_send, ret_recv):
+def kernel(kind_ref, offs_ref, q_ref, k_ref, v_ref, w_ref, out_ref,
+           snd, rcv, qx, kv0, kv1, kv2, att, ret, wbuf, fin, par, far_out, far_in, near_out, near_in, own,
+           snd_sem, rcv_sem, halo_send, halo_recv, ret_send, ret_recv,
+           wy_send, wy_recv, wr_send, wr_recv, wl_send, wl_recv, wp_send, wp_recv,
+           ex_send, ex_recv, far_send, far_recv, near_send, near_recv):
     s = lax.axis_index("seq")
     g = lax.axis_index("head")
     frame = s // 2
     half = s % 2
+    z = s // 4
+    y = s % 4
+    x = g // 2
+    core = g % 2
+    mate = {"head": x * 2 + 1 - core}
+    x_up = {"head": lax.rem(x + 1, 4) * 2 + core}
+    x_down = {"head": lax.rem(x + 3, 4) * 2 + core}
     kvs = (kv0, kv1, kv2)
 
     barrier = pltpu.get_barrier_semaphore()
@@ -37,6 +46,8 @@
         return c
 
     lax.fori_loop(1, NS, greet, 0)
+    for peer in (mate, x_up, x_down):
+        pl.semaphore_signal(barrier, inc=1, device_id=peer, device_id_type=MESH)
 
     kinds = [kind_ref[g * 3 + i] for i in range(3)]
     sp0 = kinds[0] == 0
@@ -66,7 +77,8 @@
         return c
 
     lax.fori_loop(0, 8, prep, 0)
-    pl.semaphore_wait(barrier, NS - 1)
+    wbuf[0, z, y] = w_ref[...]
+    pl.semaphore_wait(barrier, NS + 2)
 
     def scatter(slot):
         def go(i, c):
@@ -95,10 +107,6 @@
             op.start()
             ops.append(op)
         return ops
-
-    scatter(0)
-    halo2 = halo(2)
-    scatter(1)
 
     def attend(slot):
         kv = kvs[slot]
@@ -163,51 +171,152 @@
         pltpu.make_async_copy(
             att.at[slot, pl.ds(half * 2, 2), frame], ret.at[slot, s], ret_recv.at[slot]).start()
 
+    def push(src_ref, dst_ref, send, recv, peer):
+        op = pltpu.make_async_remote_copy(
+            src_ref=src_ref, dst_ref=dst_ref, send_sem=send, recv_sem=recv,
+            device_id=peer, device_id_type=MESH)
+        op.start()
+        return op
+
+    y_up = {"seq": z * 4 + lax.rem(y + 1, 4)}
+    y_down = {"seq": z * 4 + lax.rem(y + 3, 4)}
+    z_up = {"seq": lax.rem(z + 1, 8) * 4 + y}
+    z_down = {"seq": lax.rem(z + 7, 8) * 4 + y}
+
+    def w_right(t):
+        row = wbuf.at[0, lax.rem(z + 8 - t, 8)]
+        return push(row, row, wr_send.at[t], wr_recv.at[t], z_up)
+
+    def w_left(t):
+        row = wbuf.at[0, lax.rem(z + t, 8)]
+        return push(row, row, wl_send.at[t], wl_recv.at[t], z_down)
+
+    def exchange(slot):
+        return push(fin.at[slot, :, 1 - core], par.at[slot], ex_send.at[slot], ex_recv.at[slot], mate)
+
+    def settle(slot):
+        pltpu.make_async_copy(ret.at[slot], ret.at[slot], ret_recv.at[slot]).wait()
+        temporal = kind_slot[slot] == 1
+
+        def go(t, c):
+            got = ret[slot, pl.ds(t * 4, 4)].reshape(DH, DH)
+            mine = att[slot, t // 2, pl.ds((t % 2) * 8, 8)].reshape(DH, DH)
+            fin[slot, t // 2, t % 2] = pick(temporal, got, mine)
+            return c
+
+        lax.fori_loop(0, 8, go, 0)
+
+    wy0 = push(w_ref, wbuf.at[0, z, y], wy_send.at[0], wy_recv.at[0], y_up)
+    wy1 = push(w_ref, wbuf.at[0, z, y], wy_send.at[1], wy_recv.at[1], y_down)
+    scatter(0)
+    halo2 = halo(2)
+    scatter(1)
     wait_halo(halo2)
     attend(2)
+
+    def spatial(t, c):
+        fin[2, t // 2, t % 2] = att[2, t // 2, pl.ds((t % 2) * 8, 8)].reshape(DH, DH)
+        return c
+
+    lax.fori_loop(0, 8, spatial, 0)
+    ex2 = exchange(2)
     arrive(0)
     halo0 = halo(0)
+    wy0.wait_recv()
+    piece = wbuf.at[0, z, lax.rem(y + 3, 4)]
+    wy2 = push(piece, piece, wy_send.at[2], wy_recv.at[2], y_up)
     arrive(1)
     halo1 = halo(1)
+    wy1.wait_recv()
+    wy2.wait_recv()
+    rights, lefts = [w_right(0)], [w_left(0)]
     wait_halo(halo0)
     attend(0)
     give_back(0)
+    rights[0].wait_recv()
+    lefts[0].wait_recv()
+    rights.append(w_right(1))
+    lefts.append(w_left(1))
     wait_halo(halo1)
     attend(1)
     give_back(1)
-
-    def finish2(b, c):
-        out_ref[pl.ds(pl.multiple_of(b * BLK, BLK), BLK), 256:384] = att[2, b].reshape(BLK, DH)
-        return c
-
-    lax.fori_loop(0, 4, finish2, 0)
-
-    for slot in range(2):
-        pltpu.make_async_copy(ret.at[slot], ret.at[slot], ret_recv.at[slot]).wait()
-        temporal = kind_slot[slot] == 1
-
-        def fin(b, c):
-            x = pick(temporal, ret[slot, pl.ds(b * 8, 8)].reshape(BLK, DH), att[slot, b].reshape(BLK, DH))
-            out_ref[pl.ds(pl.multiple_of(b * BLK, BLK), BLK), slot * DH:(slot + 1) * DH] = x
-            return c
-
-        lax.fori_loop(0, 4, fin, 0)
+    rights[1].wait_recv()
+    lefts[1].wait_recv()
+    rights.append(w_right(2))
+    lefts.append(w_left(2))
+    settle(0)
+    ex0 = exchange(0)
+    rights[2].wait_recv()
+    lefts[2].wait_recv()
+    rights.append(w_right(3))
+    settle(1)
+    ex1 = exchange(1)
+    rights[3].wait_recv()
+    wp = push(wbuf.at[0], wbuf.at[1], wp_send, wp_recv, mate)
+    for op in (ex2, ex0, ex1):
+        op.wait_recv()
+    wp.wait_recv()
+
+    def part(dest, n):
+        total = None
+        for side in range(2):
+            if side == 0:
+                rows = [fin[i, dest, core] for i in range(3)]
+            else:
+                rows = [par[i, dest] for i in range(3)]
+            wt = wbuf[side, pl.ds(2 * n, 2)].reshape(768, 384)
+            p = lax.dot_general(jnp.concatenate(rows, axis=1), wt, (((1,), (1,)), ((), ())),
+                                preferred_element_type=F32)
+            total = p if total is None else total + p
+        return total
+
+    up, down, far = lax.rem(x + 1, 4), lax.rem(x + 3, 4), lax.rem(x + 2, 4)
+    fars = []
+    for n in (0, 2, 1, 3):
+        far_out[n] = part(far, n).astype(BF)
+        fars.append(push(far_out.at[n], far_in.at[n], far_send.at[n], far_recv.at[n], x_up if n < 2 else x_down))
+    nears = []
+    for n in range(2):
+        near_out[0, 2 + n] = part(up, 2 + n).astype(BF)
+        nears.append(push(near_out.at[0, 2 + n], near_in.at[0, 2 + n], near_send.at[0, 2 + n],
+                          near_recv.at[0, 2 + n], x_up))
+        near_out[1, n] = part(down, n).astype(BF)
+        nears.append(push(near_out.at[1, n], near_in.at[1, n], near_send.at[1, n],
+                          near_recv.at[1, n], x_down))
+    for n in range(4):
+        own[n] = part(x, n)
+    for n in range(2):
+        fars[0 if n == 0 else 2].wait_recv()
+        near_out[0, n] = (part(up, n) + far_in[n].astype(F32)).astype(BF)
+        nears.append(push(near_out.at[0, n], near_in.at[0, n], near_send.at[0, n],
+                          near_recv.at[0, n], x_up))
+        fars[1 if n == 0 else 3].wait_recv()
+        near_out[1, 2 + n] = (part(down, 2 + n) + far_in[2 + n].astype(F32)).astype(BF)
+        nears.append(push(near_out.at[1, 2 + n], near_in.at[1, 2 + n], near_send.at[1, 2 + n],
+                          near_recv.at[1, 2 + n], x_down))
+    for op in nears:
+        op.wait_recv()
+    for n in range(4):
+        total = own[n] + near_in[0, n].astype(F32) + near_in[1, n].astype(F32)
+        out_ref[:, n * 768:(n + 1) * 768] = total.astype(BF)
 
     for slot in range(2):
         sent = snd.at[slot, pl.ds(0, NS - 1)]
         pltpu.make_async_copy(sent, sent, snd_sem.at[slot]).wait()
         back = ret.at[slot, pl.ds(0, NS - 1)]
         pltpu.make_async_copy(back, back, ret_send.at[slot]).wait()
-
-
-def attention(queries, keys, values, head_kind, band_offsets):
+    for op in [wy0, wy1, wy2, wp, ex0, ex1, ex2] + rights + lefts + fars + nears:
+        op.wait_send()
+
+
+def attention(queries, keys, values, wt, head_kind, band_offsets):
     vm = pl.BlockSpec(memory_space=pltpu.VMEM)
     sm = pl.BlockSpec(memory_space=pltpu.SMEM)
     dma = pltpu.SemaphoreType.DMA
     return pl.pallas_call(
         kernel,
-        out_shape=jax.ShapeDtypeStruct((1024, 384), BF),
-        in_specs=[sm, sm, vm, vm, vm],
+        out_shape=jax.ShapeDtypeStruct((128, 3072), BF),
+        in_specs=[sm, sm, vm, vm, vm, vm],
         out_specs=vm,
         scratch_shapes=[
             pltpu.VMEM((2, NS, 3, 2, 16, DH), BF),
@@ -218,11 +327,21 @@
             pltpu.VMEM((2, 12, 16, 16, DH), BF),
             pltpu.VMEM((3, 4, 16, 16, DH), BF),
             pltpu.VMEM((2, NS, 2, 16, DH), BF),
+            pltpu.VMEM((2, 8, 4, 96, 384), BF),
+            pltpu.VMEM((3, 4, 2, DH, DH), BF),
+            pltpu.VMEM((3, 4, DH, DH), BF),
+            pltpu.VMEM((4, DH, 768), BF),
+            pltpu.VMEM((4, DH, 768), BF),
+            pltpu.VMEM((2, 4, DH, 768), BF),
+            pltpu.VMEM((2, 4, DH, 768), BF),
+            pltpu.VMEM((4, DH, 768), F32),
             dma((2,)), dma((2,)), dma((3, 2)), dma((3, 2)), dma((2,)), dma((2,)),
+            dma((3,)), dma((3,)), dma((4,)), dma((4,)), dma((3,)), dma((3,)), dma, dma,
+            dma((3,)), dma((3,)), dma((4,)), dma((4,)), dma((2, 4)), dma((2, 4)),
         ],
         compiler_params=pltpu.CompilerParams(
             collective_id=0, has_side_effects=True, vmem_limit_bytes=60 * 1024 * 1024),
-    )(head_kind, band_offsets, queries, keys, values)
+    )(head_kind, band_offsets, queries, keys, values, wt)
 
 
 def body(queries, keys, values, w_out, head_kind, band_offsets):
@@ -233,11 +352,7 @@
     sp2 = (types[0] != 0) & (types[1] != 0)
     rows = jnp.concatenate(
         [jnp.where(sp0, b, a), jnp.where(sp2, b, d), jnp.where(sp0, a, jnp.where(sp2, d, b))], axis=0)
-    weight_rows = lax.all_gather(rows, "seq", axis=1, tiled=True)
-    final_rows = attention(queries, keys, values, head_kind, band_offsets)
-    return lax.psum_scatter(
-        jnp.dot(final_rows, weight_rows, preferred_element_type=F32).astype(BF),
-        "head", scatter_dimension=0, tiled=True)
+    return attention(queries, keys, values, rows.T, head_kind, band_offsets)
 
 
 def solution(mesh):

time: 186 us -> 169 us (0.909)
  Pallas kernels: 107 us -> 162 us
  waiting for transfers between devices: 52.3 us -> 0 us
  between operations: 15.2 us -> 1.93 us
  matrix products: 8.02 us -> 0 us
  local copies, waits for them, and re-layouts: 1.31 us -> 3.38 us
    pallas_call x1, Pallas kernels: 107 us -> 162 us  [attention(): pl.pallas_call(kernel, out_shape=jax.ShapeDtypeStruct((128, 3072), BF), i...]
    reduce_scatter x1 -> x0, waiting for transfers between devices: 45.7 us -> none  [body(): lax.psum_scatter(jnp.dot(final_rows, weight_rows, preferred_element_type=...]
    dot_general x1 -> x0, matrix products: 8.02 us -> none  [body(): jnp.dot(final_rows, weight_rows, preferred_element_type=F32).astype(BF)]
    all_gather x1 -> x0, waiting for transfers between devices: 6.49 us -> none  [body(): weight_rows = lax.all_gather(rows, 'seq', axis=1, tiled=True)]
    unnamed x0 -> x3, local copies, waits for them, and re-layouts: none -> 2.72 us
  transfers between devices with their start and end apart: 2 -> 0, of which waited for: 2 -> 0; matrix products, arithmetic and copies ran while one was open for 0% -> 0% of each run, Pallas kernels for 58% -> 0%
where the time goes in v2:
time: 169 us; the launch traced here: 168 us
  Pallas kernels  162 us (96%)
  local copies, waits for them, and re-layouts  3.38 us (2%)
  between operations  1.93 us (1%)
    pallas_call x1, Pallas kernels, attention(): pl.pallas_call(kernel, out_shape=jax.ShapeDtypeStruct((128, 3072), BF), i...  162 us

profile of v2, /device:TPU:1, one launch (start us, length us, event | category | flops | bytes accessed | tf_op | source)
XLA Modules:
  0.0 168.4 jit_solution(3519460084747930953)
XLA Ops:
  0.0 0.0 copy-start
  0.0 0.7 copy-done
  0.7 0.1 dynamic_slice.3
  0.7 0.6 fusion
  3.2 0.8 broadcast_select_fusion.1
  4.0 0.6 maximum_bitcast_fusion.w_ref
  4.7 161.7 %shard_map.64 = bf16[128,3072]{1,0:T(8,128)(2,1)} custom-call(s32[24]{0:T(128)} %kind_ref.1, s32[2,7]{1,0:T(2,128)} %offs_ref.1, bf16[1024,384]{1,0:T(8,128)(2,1)} %q_ref.1, bf16[1024,384]{1,0:T(8,128)(2,1)} %k_ref.1, bf16[1024,384]{1,0:T(8,128)(2,1)} %v_ref.1, bf16[96,384]{1,0:T(8,128)(2,1)} %maximum_bitcast_fusion.w_ref), custom_call_target="tpu_custom_call" | custom-call | tf_op jit(solution)/shard_map/pallas_call | solution.py:316
  166.3 2.1 %copy.8 = bf16[128,3072]{1,0:T(8,128)(2,1)} copy(bf16[128,3072]{1,0:T(8,128)(2,1)} %shard_map.64) | data formatting | bytes 1572864
Async XLA Ops:
  0.0 0.7 copy-start

commit v3 on v2

--- a/solution.py
+++ b/solution.py
@@ -22,8 +22,8 @@
 
 
 def kernel(kind_ref, offs_ref, q_ref, k_ref, v_ref, w_ref, out_ref,
-           snd, rcv, qx, kv0, kv1, kv2, att, ret, wbuf, fin, par, far_out, far_in, near_out, near_in, own,
-           snd_sem, rcv_sem, halo_send, halo_recv, ret_send, ret_recv,
+           snd, rcv, qx, kv0, kv1, kv2, att, ret, wbuf, rly, fin, par, far_out, far_in, near_out, near_in, own,
+           snd_sem, rcv_sem, halo_send, halo_recv, rly_send, rly_recv, fwd_send, ret_send, ret_recv,
            wy_send, wy_recv, wr_send, wr_recv, wl_send, wl_recv, wp_send, wp_recv,
            ex_send, ex_recv, far_send, far_recv, near_send, near_recv):
     s = lax.axis_index("seq")
@@ -77,7 +77,13 @@
         return c
 
     lax.fori_loop(0, 8, prep, 0)
-    wbuf[0, z, y] = w_ref[...]
+    wa, wb, wd = w_ref[0:DH], w_ref[DH:2 * DH], w_ref[2 * DH:]
+    w_rows = jnp.concatenate(
+        [pick(sp0, wb, wa), pick(sp2, wb, wd), pick(sp0, wa, pick(sp2, wd, wb))], axis=0)
+    eye = (lax.broadcasted_iota(jnp.int32, (96, 96), 0)
+           == lax.broadcasted_iota(jnp.int32, (96, 96), 1)).astype(F32).astype(BF)
+    wbuf[0, z, y] = lax.dot_general(
+        eye, w_rows, (((1,), (1,)), ((), ())), preferred_element_type=F32).astype(BF)
     pl.semaphore_wait(barrier, NS + 2)
 
     def scatter(slot):
@@ -93,20 +99,53 @@
         pltpu.make_async_copy(
             snd.at[slot, s], rcv.at[slot, :, pl.ds(half * 2, 2), frame], rcv_sem.at[slot]).start()
 
+    edge = (y == 3, y == 0)
+    hop = (1, NS - 1)
+    lows = (0, 8)
+
     def halo(slot):
         kv = kvs[slot]
-        ops = []
         for side in range(2):
-            peer = lax.rem(s + (1 if side == 0 else NS - 1), NS)
-            lo = 0 if side == 0 else 8
-            op = pltpu.make_async_remote_copy(
-                src_ref=kv.at[:, pl.ds(4, 4)],
-                dst_ref=kv.at[:, pl.ds(lo, 4)],
+            lo = lows[side]
+            peer = lax.rem(s + hop[side], NS)
+            pltpu.make_async_remote_copy(
+                src_ref=kv.at[:, pl.ds(4, 2)], dst_ref=kv.at[:, pl.ds(lo, 2)],
                 send_sem=halo_send.at[slot, side], recv_sem=halo_recv.at[slot, side],
-                device_id={"seq": peer}, device_id_type=MESH)
-            op.start()
-            ops.append(op)
-        return ops
+                device_id={"seq": peer}, device_id_type=MESH).start()
+
+            @pl.when(jnp.logical_not(edge[side]))
+            def _():
+                pltpu.make_async_remote_copy(
+                    src_ref=kv.at[:, pl.ds(6, 2)], dst_ref=kv.at[:, pl.ds(lo + 2, 2)],
+                    send_sem=halo_send.at[slot, side], recv_sem=halo_recv.at[slot, side],
+                    device_id={"seq": peer}, device_id_type=MESH).start()
+
+            @pl.when(edge[side])
+            def _():
+                pltpu.make_async_remote_copy(
+                    src_ref=kv.at[:, pl.ds(6, 2)], dst_ref=rly.at[slot],
+                    send_sem=halo_send.at[slot, side], recv_sem=rly_recv.at[slot],
+                    device_id={"seq": z * 4 + (0 if side == 0 else 3)}, device_id_type=MESH).start()
+
+    def relay(slot):
+        kv = kvs[slot]
+        for side in range(2):
+            lo = lows[side]
+
+            @pl.when(edge[1 - side])
+            def _():
+                pltpu.make_async_copy(rly.at[slot], rly.at[slot], rly_recv.at[slot]).wait()
+                pltpu.make_async_remote_copy(
+                    src_ref=rly.at[slot], dst_ref=kv.at[:, pl.ds(lo + 2, 2)],
+                    send_sem=fwd_send.at[slot], recv_sem=halo_recv.at[slot, side],
+                    device_id={"seq": lax.rem(z + (1 if side == 0 else 7), 8) * 4 + y},
+                    device_id_type=MESH).start()
+
+    def wait_halo(slot):
+        kv = kvs[slot]
+        for side in range(2):
+            got = kv.at[:, pl.ds(lows[side], 4)]
+            pltpu.make_async_copy(got, got, halo_recv.at[slot, side]).wait()
 
     def attend(slot):
         kv = kvs[slot]
@@ -138,12 +177,10 @@
 
         lax.fori_loop(0, 4, block, 0)
 
-    def wait_halo(ops):
-        for op in ops:
-            op.wait()
-
-    def arrive(slot):
+    def wait_slot(slot):
         pltpu.make_async_copy(rcv.at[slot], rcv.at[slot], rcv_sem.at[slot]).wait()
+
+    def choose(slot):
         temporal = kind_slot[slot] == 1
 
         def sel(b, c):
@@ -206,12 +243,42 @@
 
         lax.fori_loop(0, 8, go, 0)
 
-    wy0 = push(w_ref, wbuf.at[0, z, y], wy_send.at[0], wy_recv.at[0], y_up)
-    wy1 = push(w_ref, wbuf.at[0, z, y], wy_send.at[1], wy_recv.at[1], y_down)
+    passed = []
+
+    def pass_row(r):
+        passed.append(push(wbuf.at[0, r], wbuf.at[1, r], wp_send.at[len(passed)], wp_recv.at[r], mate))
+
+    def z_step(t):
+        if t > 0:
+            rights[t - 1].wait_recv()
+            if t <= 3:
+                lefts[t - 1].wait_recv()
+        if t < 4:
+            rights.append(w_right(t))
+        if t < 3:
+            lefts.append(w_left(t))
+        if t > 0:
+            pass_row(lax.rem(z + 8 - t, 8))
+            if t <= 3:
+                pass_row(lax.rem(z + t, 8))
+        else:
+            pass_row(z)
+
+    rights, lefts = [], []
+    mine = wbuf.at[0, z, y]
     scatter(0)
-    halo2 = halo(2)
+    halo(2)
+    wy0 = push(mine, mine, wy_send.at[0], wy_recv.at[0], y_up)
+    wy1 = push(mine, mine, wy_send.at[1], wy_recv.at[1], y_down)
+    relay(2)
+    wait_slot(0)
     scatter(1)
-    wait_halo(halo2)
+    choose(0)
+    halo(0)
+    wy0.wait_recv()
+    piece = wbuf.at[0, z, lax.rem(y + 3, 4)]
+    wy2 = push(piece, piece, wy_send.at[2], wy_recv.at[2], y_up)
+    wait_halo(2)
     attend(2)
 
     def spatial(t, c):
@@ -220,42 +287,33 @@
 
     lax.fori_loop(0, 8, spatial, 0)
     ex2 = exchange(2)
-    arrive(0)
-    halo0 = halo(0)
-    wy0.wait_recv()
-    piece = wbuf.at[0, z, lax.rem(y + 3, 4)]
-    wy2 = push(piece, piece, wy_send.at[2], wy_recv.at[2], y_up)
-    arrive(1)
-    halo1 = halo(1)
+    relay(0)
+    wait_slot(1)
+    choose(1)
+    halo(1)
     wy1.wait_recv()
     wy2.wait_recv()
-    rights, lefts = [w_right(0)], [w_left(0)]
-    wait_halo(halo0)
+    z_step(0)
+    wait_halo(0)
     attend(0)
+    relay(1)
+    z_step(1)
+    wait_halo(1)
     give_back(0)
-    rights[0].wait_recv()
-    lefts[0].wait_recv()
-    rights.append(w_right(1))
-    lefts.append(w_left(1))
-    wait_halo(halo1)
     attend(1)
     give_back(1)
-    rights[1].wait_recv()
-    lefts[1].wait_recv()
-    rights.append(w_right(2))
-    lefts.append(w_left(2))
+    z_step(2)
     settle(0)
     ex0 = exchange(0)
-    rights[2].wait_recv()
-    lefts[2].wait_recv()
-    rights.append(w_right(3))
+    z_step(3)
     settle(1)
     ex1 = exchange(1)
-    rights[3].wait_recv()
-    wp = push(wbuf.at[0], wbuf.at[1], wp_send, wp_recv, mate)
+    z_step(4)
     for op in (ex2, ex0, ex1):
         op.wait_recv()
-    wp.wait_recv()
+    for r in range(8):
+        row = wbuf.at[1, r]
+        pltpu.make_async_copy(row, row, wp_recv.at[r]).wait()
 
     def part(dest, n):
         total = None
@@ -305,7 +363,16 @@
         pltpu.make_async_copy(sent, sent, snd_sem.at[slot]).wait()
         back = ret.at[slot, pl.ds(0, NS - 1)]
         pltpu.make_async_copy(back, back, ret_send.at[slot]).wait()
-    for op in [wy0, wy1, wy2, wp, ex0, ex1, ex2] + rights + lefts + fars + nears:
+    for slot in range(3):
+        kv = kvs[slot]
+        for side in range(2):
+            out = kv.at[:, pl.ds(4, 4)]
+            pltpu.make_async_copy(out, out, halo_send.at[slot, side]).wait()
+
+            @pl.when(edge[1 - side])
+            def _():
+                pltpu.make_async_copy(rly.at[slot], rly.at[slot], fwd_send.at[slot]).wait()
+    for op in [wy0, wy1, wy2, ex0, ex1, ex2] + passed + rights + lefts + fars + nears:
         op.wait_send()
 
 
@@ -328,6 +395,7 @@
             pltpu.VMEM((3, 4, 16, 16, DH), BF),
             pltpu.VMEM((2, NS, 2, 16, DH), BF),
             pltpu.VMEM((2, 8, 4, 96, 384), BF),
+            pltpu.VMEM((3, 2, 2, 16, 16, DH), BF),
             pltpu.VMEM((3, 4, 2, DH, DH), BF),
             pltpu.VMEM((3, 4, DH, DH), BF),
             pltpu.VMEM((4, DH, 768), BF),
@@ -335,8 +403,9 @@
             pltpu.VMEM((2, 4, DH, 768), BF),
             pltpu.VMEM((2, 4, DH, 768), BF),
             pltpu.VMEM((4, DH, 768), F32),
-            dma((2,)), dma((2,)), dma((3, 2)), dma((3, 2)), dma((2,)), dma((2,)),
-            dma((3,)), dma((3,)), dma((4,)), dma((4,)), dma((3,)), dma((3,)), dma, dma,
+            dma((2,)), dma((2,)), dma((3, 2)), dma((3, 2)), dma((3,)), dma((3,)), dma((3,)),
+            dma((2,)), dma((2,)),
+            dma((3,)), dma((3,)), dma((4,)), dma((4,)), dma((3,)), dma((3,)), dma((8,)), dma((8,)),
             dma((3,)), dma((3,)), dma((4,)), dma((4,)), dma((2, 4)), dma((2, 4)),
         ],
         compiler_params=pltpu.CompilerParams(
@@ -345,14 +414,7 @@
 
 
 def body(queries, keys, values, w_out, head_kind, band_offsets):
-    head_rank = lax.axis_index("head")
-    types = lax.dynamic_slice_in_dim(head_kind, head_rank * 3, 3)
-    a, b, d = w_out[0:DH], w_out[DH:2 * DH], w_out[2 * DH:]
-    sp0 = types[0] == 0
-    sp2 = (types[0] != 0) & (types[1] != 0)
-    rows = jnp.concatenate(
-        [jnp.where(sp0, b, a), jnp.where(sp2, b, d), jnp.where(sp0, a, jnp.where(sp2, d, b))], axis=0)
-    return attention(queries, keys, values, rows.T, head_kind, band_offsets)
+    return attention(queries, keys, values, w_out, head_kind, band_offsets)
 
 
 def solution(mesh):

time: 169 us -> 146 us (0.86)
  Pallas kernels: 162 us -> 141 us
  between operations: 1.93 us -> 0.01 us
    pallas_call x1, Pallas kernels: 162 us -> 141 us  [attention(): pl.pallas_call(kernel, out_shape=jax.ShapeDtypeStruct((128, 3072), BF), i...]
    unnamed x3 -> x2, local copies, waits for them, and re-layouts: 2.72 us -> 3.69 us
where the time goes in v3:
time: 146 us; the launch traced here: 145 us
  Pallas kernels  141 us (97%)
  local copies, waits for them, and re-layouts  3.69 us (3%)
    pallas_call x1, Pallas kernels, attention(): pl.pallas_call(kernel, out_shape=jax.ShapeDtypeStruct((128, 3072), BF), i...  141 us
    unnamed x2, local copies, waits for them, and re-layouts  3.69 us

profile of v3, /device:TPU:1, one launch (start us, length us, event | category | flops | bytes accessed | tf_op | source)
XLA Modules:
  0.0 144.6 jit_solution(13031267486119452692)
XLA Ops:
  0.0 1.6 %copy.7.w_ref = bf16[384,96]{1,0:T(8,128)(2,1)} copy(bf16[384,96]{0,1:T(8,128)(2,1)} %param.9) | data formatting | bytes 147456 | tf_op args[3]
  1.6 140.9 %shard_map.64 = bf16[128,3072]{1,0:T(8,128)(2,1)} custom-call(s32[24]{0:T(128)} %kind_ref.1, s32[2,7]{1,0:T(2,128)} %offs_ref.1, bf16[1024,384]{1,0:T(8,128)(2,1)} %q_ref.1, bf16[1024,384]{1,0:T(8,128)(2,1)} %k_ref.1, bf16[1024,384]{1,0:T(8,128)(2,1)} %v_ref.1, bf16[384,96]{1,0:T(8,128)(2,1)} %copy.7.w_ref), custom_call_target="tpu_custom_call" | custom-call | tf_op jit(solution)/shard_map/pallas_call | solution.py:383
  142.6 2.1 %copy.9 = bf16[128,3072]{1,0:T(8,128)(2,1)} copy(bf16[128,3072]{1,0:T(8,128)(2,1)} %shard_map.64) | data formatting | bytes 1572864

commit v4 on v3

--- a/solution.py
+++ b/solution.py
@@ -147,7 +147,7 @@
             got = kv.at[:, pl.ds(lows[side], 4)]
             pltpu.make_async_copy(got, got, halo_recv.at[slot, side]).wait()
 
-    def attend(slot):
+    def attend(slot, first=0, last=4):
         kv = kvs[slot]
         offs = [jnp.where(kind_slot[slot] == 1, offs_ref[1, o], offs_ref[0, o]) for o in range(KOFF)]
         ones = jnp.ones((BLK, DH), BF)
@@ -175,7 +175,7 @@
             att[slot, j] = o.reshape(16, 16, DH)
             return c
 
-        lax.fori_loop(0, 4, block, 0)
+        lax.fori_loop(first, last, block, 0)
 
     def wait_slot(slot):
         pltpu.make_async_copy(rcv.at[slot], rcv.at[slot], rcv_sem.at[slot]).wait()
@@ -195,18 +195,29 @@
 
         lax.fori_loop(0, 4, sel, 0)
 
-    def give_back(slot):
+    def give_back(slot, side):
         def go(i, c):
-            d = lax.rem(s + i, NS)
+            to = lax.rem(frame + i, 16)
             pltpu.make_async_remote_copy(
-                src_ref=att.at[slot, pl.ds((d % 2) * 2, 2), d // 2],
+                src_ref=att.at[slot, side * 2:side * 2 + 2, to],
                 dst_ref=ret.at[slot, s],
                 send_sem=ret_send.at[slot], recv_sem=ret_recv.at[slot],
-                device_id={"seq": d}, device_id_type=MESH).start()
+                device_id={"seq": to * 2 + side}, device_id_type=MESH).start()
             return c
-        lax.fori_loop(1, NS, go, 0)
-        pltpu.make_async_copy(
-            att.at[slot, pl.ds(half * 2, 2), frame], ret.at[slot, s], ret_recv.at[slot]).start()
+        lax.fori_loop(1, 16, go, 0)
+
+        @pl.when(half == side)
+        def _():
+            pltpu.make_async_copy(
+                att.at[slot, side * 2:side * 2 + 2, frame], ret.at[slot, s], ret_recv.at[slot]).start()
+
+        @pl.when(half != side)
+        def _():
+            pltpu.make_async_remote_copy(
+                src_ref=att.at[slot, side * 2:side * 2 + 2, frame],
+                dst_ref=ret.at[slot, s],
+                send_sem=ret_send.at[slot], recv_sem=ret_recv.at[slot],
+                device_id={"seq": frame * 2 + side}, device_id_type=MESH).start()
 
     def push(src_ref, dst_ref, send, recv, peer):
         op = pltpu.make_async_remote_copy(
@@ -221,11 +232,11 @@
     z_down = {"seq": lax.rem(z + 7, 8) * 4 + y}
 
     def w_right(t):
-        row = wbuf.at[0, lax.rem(z + 8 - t, 8)]
+        row = wbuf.at[0, lax.rem(z + 8 - t, 8), y]
         return push(row, row, wr_send.at[t], wr_recv.at[t], z_up)
 
     def w_left(t):
-        row = wbuf.at[0, lax.rem(z + t, 8)]
+        row = wbuf.at[0, lax.rem(z + t, 8), y]
         return push(row, row, wl_send.at[t], wl_recv.at[t], z_down)
 
     def exchange(slot):
@@ -244,9 +255,11 @@
         lax.fori_loop(0, 8, go, 0)
 
     passed = []
-
-    def pass_row(r):
-        passed.append(push(wbuf.at[0, r], wbuf.at[1, r], wp_send.at[len(passed)], wp_recv.at[r], mate))
+    columns = (y, lax.rem(y + 3, 4), lax.rem(y + 1, 4), lax.rem(y + 2, 4))
+
+    def pass_column(i):
+        passed.append(push(wbuf.at[0, :, columns[i]], wbuf.at[1, :, columns[i]],
+                           wp_send.at[i], wp_recv.at[i], mate))
 
     def z_step(t):
         if t > 0:
@@ -257,27 +270,37 @@
             rights.append(w_right(t))
         if t < 3:
             lefts.append(w_left(t))
-        if t > 0:
-            pass_row(lax.rem(z + 8 - t, 8))
-            if t <= 3:
-                pass_row(lax.rem(z + t, 8))
+
+    def y_step(t):
+        if t == 0:
+            part = wbuf.at[0, :, y]
+            ys.append(push(part, part, wy_send.at[0], wy_recv.at[0], y_up))
+            ys.append(push(part, part, wy_send.at[1], wy_recv.at[1], y_down))
+            pass_column(0)
+        elif t == 1:
+            ys[0].wait_recv()
+            part = wbuf.at[0, pl.ds(0, 4), columns[1]]
+            ys.append(push(part, part, wy_send.at[2], wy_recv.at[2], y_up))
+            ys[1].wait_recv()
+            part = wbuf.at[0, pl.ds(4, 4), columns[2]]
+            ys.append(push(part, part, wy_send.at[3], wy_recv.at[3], y_down))
+            pass_column(1)
+            pass_column(2)
         else:
-            pass_row(z)
-
-    rights, lefts = [], []
-    mine = wbuf.at[0, z, y]
+            ys[2].wait_recv()
+            ys[3].wait_recv()
+            pass_column(3)
+
+    rights, lefts, ys = [], [], []
     scatter(0)
+    z_step(0)
     halo(2)
-    wy0 = push(mine, mine, wy_send.at[0], wy_recv.at[0], y_up)
-    wy1 = push(mine, mine, wy_send.at[1], wy_recv.at[1], y_down)
     relay(2)
     wait_slot(0)
     scatter(1)
     choose(0)
     halo(0)
-    wy0.wait_recv()
-    piece = wbuf.at[0, z, lax.rem(y + 3, 4)]
-    wy2 = push(piece, piece, wy_send.at[2], wy_recv.at[2], y_up)
+    z_step(1)
     wait_halo(2)
     attend(2)
 
@@ -287,33 +310,35 @@
 
     lax.fori_loop(0, 8, spatial, 0)
     ex2 = exchange(2)
+    z_step(2)
     relay(0)
     wait_slot(1)
     choose(1)
     halo(1)
-    wy1.wait_recv()
-    wy2.wait_recv()
-    z_step(0)
+    z_step(3)
     wait_halo(0)
-    attend(0)
+    attend(0, 0, 2)
+    give_back(0, 0)
     relay(1)
-    z_step(1)
+    attend(0, 2, 4)
+    give_back(0, 1)
+    z_step(4)
+    y_step(0)
     wait_halo(1)
-    give_back(0)
-    attend(1)
-    give_back(1)
-    z_step(2)
+    attend(1, 0, 2)
+    give_back(1, 0)
+    attend(1, 2, 4)
+    give_back(1, 1)
+    y_step(1)
     settle(0)
     ex0 = exchange(0)
-    z_step(3)
     settle(1)
     ex1 = exchange(1)
-    z_step(4)
+    y_step(2)
     for op in (ex2, ex0, ex1):
         op.wait_recv()
-    for r in range(8):
-        row = wbuf.at[1, r]
-        pltpu.make_async_copy(row, row, wp_recv.at[r]).wait()
+    for op in passed:
+        op.wait_recv()
 
     def part(dest, n):
         total = None
@@ -372,7 +397,7 @@
             @pl.when(edge[1 - side])
             def _():
                 pltpu.make_async_copy(rly.at[slot], rly.at[slot], fwd_send.at[slot]).wait()
-    for op in [wy0, wy1, wy2, ex0, ex1, ex2] + passed + rights + lefts + fars + nears:
+    for op in [ex0, ex1, ex2] + ys + passed + rights + lefts + fars + nears:
         op.wait_send()
 
 
@@ -405,7 +430,7 @@
             pltpu.VMEM((4, DH, 768), F32),
             dma((2,)), dma((2,)), dma((3, 2)), dma((3, 2)), dma((3,)), dma((3,)), dma((3,)),
             dma((2,)), dma((2,)),
-            dma((3,)), dma((3,)), dma((4,)), dma((4,)), dma((3,)), dma((3,)), dma((8,)), dma((8,)),
+            dma((4,)), dma((4,)), dma((4,)), dma((4,)), dma((3,)), dma((3,)), dma((4,)), dma((4,)),
             dma((3,)), dma((3,)), dma((4,)), dma((4,)), dma((2, 4)), dma((2, 4)),
         ],
         compiler_params=pltpu.CompilerParams(

time: 146 us -> 140 us (0.959)
  Pallas kernels: 141 us -> 136 us
    pallas_call x1, Pallas kernels: 141 us -> 136 us  [attention(): pl.pallas_call(kernel, out_shape=jax.ShapeDtypeStruct((128, 3072), BF), i...]
where the time goes in v4:
time: 140 us; the launch traced here: 139 us
  Pallas kernels  136 us (97%)
  local copies, waits for them, and re-layouts  3.69 us (3%)
    pallas_call x1, Pallas kernels, attention(): pl.pallas_call(kernel, out_shape=jax.ShapeDtypeStruct((128, 3072), BF), i...  136 us
    unnamed x2, local copies, waits for them, and re-layouts  3.69 us

profile of v4, /device:TPU:1, one launch (start us, length us, event | category | flops | bytes accessed | tf_op | source)
XLA Modules:
  0.0 139.3 jit_solution(10130625736773936284)
XLA Ops:
  0.0 1.6 %copy.7.w_ref = bf16[384,96]{1,0:T(8,128)(2,1)} copy(bf16[384,96]{0,1:T(8,128)(2,1)} %param.9) | data formatting | bytes 147456 | tf_op args[3]
  1.6 135.6 %shard_map.64 = bf16[128,3072]{1,0:T(8,128)(2,1)} custom-call(s32[24]{0:T(128)} %kind_ref.1, s32[2,7]{1,0:T(2,128)} %offs_ref.1, bf16[1024,384]{1,0:T(8,128)(2,1)} %q_ref.1, bf16[1024,384]{1,0:T(8,128)(2,1)} %k_ref.1, bf16[1024,384]{1,0:T(8,128)(2,1)} %v_ref.1, bf16[384,96]{1,0:T(8,128)(2,1)} %copy.7.w_ref), custom_call_target="tpu_custom_call" | custom-call | tf_op jit(solution)/shard_map/pallas_call | solution.py:408
  137.2 2.1 %copy.9 = bf16[128,3072]{1,0:T(8,128)(2,1)} copy(bf16[128,3072]{1,0:T(8,128)(2,1)} %shard_map.64) | data formatting | bytes 1572864

commit v5 on v4

--- a/solution.py
+++ b/solution.py
@@ -298,9 +298,10 @@
     relay(2)
     wait_slot(0)
     scatter(1)
+    z_step(1)
     choose(0)
     halo(0)
-    z_step(1)
+    z_step(2)
     wait_halo(2)
     attend(2)
 
@@ -310,20 +311,19 @@
 
     lax.fori_loop(0, 8, spatial, 0)
     ex2 = exchange(2)
-    z_step(2)
+    z_step(3)
     relay(0)
     wait_slot(1)
     choose(1)
     halo(1)
-    z_step(3)
+    z_step(4)
+    y_step(0)
     wait_halo(0)
     attend(0, 0, 2)
     give_back(0, 0)
     relay(1)
     attend(0, 2, 4)
     give_back(0, 1)
-    z_step(4)
-    y_step(0)
     wait_halo(1)
     attend(1, 0, 2)
     give_back(1, 0)

time: 140 us -> 138 us (0.986)
  Pallas kernels: 136 us -> 132 us
    pallas_call x1, Pallas kernels: 136 us -> 132 us  [attention(): pl.pallas_call(kernel, out_shape=jax.ShapeDtypeStruct((128, 3072), BF), i...]
where the time goes in v5:
time: 138 us; the launch traced here: 136 us
  Pallas kernels  132 us (96%)
  local copies, waits for them, and re-layouts  3.69 us (3%)
    pallas_call x1, Pallas kernels, attention(): pl.pallas_call(kernel, out_shape=jax.ShapeDtypeStruct((128, 3072), BF), i...  132 us
    unnamed x2, local copies, waits for them, and re-layouts  3.69 us

profile of v5, /device:TPU:1, one launch (start us, length us, event | category | flops | bytes accessed | tf_op | source)
XLA Modules:
  0.0 136.2 jit_solution(8873473318452272637)
XLA Ops:
  0.0 1.6 %copy.7.w_ref = bf16[384,96]{1,0:T(8,128)(2,1)} copy(bf16[384,96]{0,1:T(8,128)(2,1)} %param.9) | data formatting | bytes 147456 | tf_op args[3]
  1.6 132.5 %shard_map.64 = bf16[128,3072]{1,0:T(8,128)(2,1)} custom-call(s32[24]{0:T(128)} %kind_ref.1, s32[2,7]{1,0:T(2,128)} %offs_ref.1, bf16[1024,384]{1,0:T(8,128)(2,1)} %q_ref.1, bf16[1024,384]{1,0:T(8,128)(2,1)} %k_ref.1, bf16[1024,384]{1,0:T(8,128)(2,1)} %v_ref.1, bf16[384,96]{1,0:T(8,128)(2,1)} %copy.7.w_ref), custom_call_target="tpu_custom_call" | custom-call | tf_op jit(solution)/shard_map/pallas_call | solution.py:408
  134.1 2.1 %copy.9 = bf16[128,3072]{1,0:T(8,128)(2,1)} copy(bf16[128,3072]{1,0:T(8,128)(2,1)} %shard_map.64) | data formatting | bytes 1572864

commit v6 on v5

--- a/solution.py
+++ b/solution.py
@@ -327,9 +327,9 @@
     wait_halo(1)
     attend(1, 0, 2)
     give_back(1, 0)
+    y_step(1)
     attend(1, 2, 4)
     give_back(1, 1)
-    y_step(1)
     settle(0)
     ex0 = exchange(0)
     settle(1)

time: 138 us -> 139 us (level)
  Pallas kernels: 132 us -> 134 us
where the time goes in v6:
time: 139 us; the launch traced here: 137 us
  Pallas kernels  134 us (96%)
  local copies, waits for them, and re-layouts  3.69 us (3%)
    pallas_call x1, Pallas kernels, attention(): pl.pallas_call(kernel, out_shape=jax.ShapeDtypeStruct((128, 3072), BF), i...  134 us
    unnamed x2, local copies, waits for them, and re-layouts  3.69 us

profile of v6, /device:TPU:1, one launch (start us, length us, event | category | flops | bytes accessed | tf_op | source)
XLA Modules:
  0.0 137.2 jit_solution(13077144130389214063)
XLA Ops:
  0.0 1.6 %copy.7.w_ref = bf16[384,96]{1,0:T(8,128)(2,1)} copy(bf16[384,96]{0,1:T(8,128)(2,1)} %param.9) | data formatting | bytes 147456 | tf_op args[3]
  1.6 133.5 %shard_map.64 = bf16[128,3072]{1,0:T(8,128)(2,1)} custom-call(s32[24]{0:T(128)} %kind_ref.1, s32[2,7]{1,0:T(2,128)} %offs_ref.1, bf16[1024,384]{1,0:T(8,128)(2,1)} %q_ref.1, bf16[1024,384]{1,0:T(8,128)(2,1)} %k_ref.1, bf16[1024,384]{1,0:T(8,128)(2,1)} %v_ref.1, bf16[384,96]{1,0:T(8,128)(2,1)} %copy.7.w_ref), custom_call_target="tpu_custom_call" | custom-call | tf_op jit(solution)/shard_map/pallas_call | solution.py:408
  135.1 2.1 %copy.9 = bf16[128,3072]{1,0:T(8,128)(2,1)} copy(bf16[128,3072]{1,0:T(8,128)(2,1)} %shard_map.64) | data formatting | bytes 1572864
